TPU v7x, 32 devices: a whole 2x2x4 slice. The times are simulated.
32 devices in a mesh: layer: 4 (over y, core), feat: 8 (over z, x).
Axes of the slice: x: 2, y: 2, z: 4, core: 2. Of those that a mesh axis runs over, the one named last changes fastest.
Arguments:
- acts: bfloat16 [4, 384, 2048], P('layer', 'feat'), may hold values from -64 to 64
- errors: bfloat16 [4, 384, 2048], P('layer', 'feat'), may hold values from -2.390625 to 2.390625
- enc_weight: bfloat16 [4, 2048, 8192], P('layer', None, 'feat'), may hold values from -0.0625 to 0.0625
- dec_weight: bfloat16 [4, 8192, 2048], P('layer', 'feat'), may hold values from -0.125 to 0.125
- chosen: int32 [384, 32], replicated, may hold values from 0 to 8191, all different within a row
Outputs:
- dec_grad: bfloat16 [4, 8192, 2048], P('layer', 'feat')
- enc_grad: bfloat16 [4, 2048, 8192], P('layer', None, 'feat')
Inputs may be any that keep to these rules, and one draw needn't show every extreme that they name: `chosen`: each row names 32 different features.
All inputs are finite; a program needn't handle non-finite values.
Results may differ from a plain program's by a relative error of at most 0.02.
Values may be sent and summed in bfloat16 or wider, within the bound.
No kernel may reach another device: no remote copies, remote signals or barrier semaphores. Data moves between devices by JAX's collectives and lax.ppermute only.
A program may use at most 64 MiB of HBM per device.

v0:
```python
import jax
import jax.numpy as jnp
from jax import lax
from jax.sharding import PartitionSpec as P


def slot_match(target, feat_dev):
    column_ids = jnp.arange(feat_dev, dtype=jnp.int32)
    return target[:, :, None] == column_ids[None, None, :]


def on_device(acts, errors, enc_weight, dec_weight, chosen):
    all_acts, all_errors = (
        lax.all_gather(acts, "feat", axis=1, tiled=True),
        lax.all_gather(errors, "feat", axis=1, tiled=True),
    )
    tokens = all_acts.shape[1]
    width = all_acts.shape[2]
    feat_dev = enc_weight.shape[2]
    first = lax.axis_index("feat") * feat_dev
    local_ids = chosen - first
    inside = (local_ids >= 0) & (local_ids < feat_dev)
    target = jnp.where(inside, local_ids, feat_dev)
    mask = jnp.any(slot_match(target, feat_dev), axis=1).astype(jnp.float32)
    squares = jnp.sum(jnp.square(all_acts.astype(jnp.float32)), axis=(1, 2))
    scale = 2.0 / (squares / (tokens * width) + 1e-06)
    partial_value = jnp.einsum(
        "ltd,ldf->tf", all_acts, enc_weight, preferred_element_type=jnp.float32
    )
    pre = lax.psum(partial_value.astype(jnp.bfloat16), "layer").astype(jnp.float32)
    codes = (pre * mask).astype(jnp.bfloat16)
    delta = (all_errors.astype(jnp.float32) * scale[:, None, None]).astype(jnp.bfloat16)
    dec_grad = jnp.einsum("tf,ltd->lfd", codes, delta, preferred_element_type=jnp.float32).astype(
        jnp.bfloat16
    )
    grad_partial = jnp.einsum("ltd,lfd->tf", delta, dec_weight, preferred_element_type=jnp.float32)
    code_grad = lax.psum(grad_partial.astype(jnp.bfloat16), "layer").astype(jnp.float32)
    pre_grad = (code_grad * mask).astype(jnp.bfloat16)
    enc_grad = jnp.einsum(
        "ltd,tf->ldf", all_acts, pre_grad, preferred_element_type=jnp.float32
    ).astype(jnp.bfloat16)
    return (dec_grad, enc_grad)


def solution(mesh):
    return jax.shard_map(
        on_device,
        mesh=mesh,
        in_specs=(
            P("layer", "feat", None),
            P("layer", "feat", None),
            P("layer", None, "feat"),
            P("layer", "feat", None),
            P(),
        ),
        out_specs=(P("layer", "feat", None), P("layer", None, "feat")),
        check_vma=False,
    )
```

profile of v0, /device:TPU:0, one launch (start us, length us, event | category | flops | bytes accessed | tf_op | source)
XLA Modules:
  0.0 178.2 jit_solution(6338268189235986830)
XLA Ops:
  7.2 0.0 all-gather.5.cloned.1.call-start
  7.2 0.7 all-gather.5.cloned.1.call-update
  7.9 0.0 all-gather.3.cloned.1.call-start
  7.9 0.7 all-gather.3.cloned.1.call-update
  8.6 0.0 all-reduce.3.cloned.1.call-start
  8.7 48.4 %all-gather.5.cloned.1.call-done = bf16[1,384,2048]{2,1,0:T(8,128)(2,1)} async-done(((bf16[1,48,2048]{2,1,0:T(8,128)(2,1)}), bf16[1,384,2048]{2,1,0:T(8,128)(2,1)}) %all-gather.5.cloned.1.call-update) | async-done | bytes 1572880 | tf_op jit(solution)/shard_map/all_gather | solution.py:14
  57.1 2.8 %multiply_reduce_fusion = f32[]{:T(128)} fusion(bf16[1,384,2048]{2,1,0:T(8,128)(2,1)} %all-gather.5.cloned.1.call-done), kind=kLoop, calls=%fused_computation.9 | loop fusion | flops 2359295 | bytes 1572868 | tf_op jit(solution)/shard_map/reduce_sum | solution.py:25
  60.6 5.3 %fusion.8 = bf16[384,1024]{1,0:T(8,128)(2,1)} fusion(bf16[1,2048,1024]{2,1,0:T(8,128)(2,1)} %param.7, bf16[1,384,2048]{2,1,0:T(8,128)(2,1)} %all-gather.5.cloned.1.call-done), kind=kOutput, calls=%fused_computation.15 | convolution fusion | flops 1611005952 | bytes 6553600 | tf_op jit(solution)/shard_map/ltd,ldf->tf/dot_general | solution.py:27
  65.9 0.0 copy-start.1
  65.9 35.9 %all-gather.3.cloned.1.call-done = bf16[1,384,2048]{2,1,0:T(8,128)(2,1)} async-done(((bf16[1,48,2048]{2,1,0:T(8,128)(2,1)}), bf16[1,384,2048]{2,1,0:T(8,128)(2,1)}) %all-gather.3.cloned.1.call-update) | async-done | bytes 1572880 | tf_op jit(solution)/shard_map/all_gather | solution.py:15
  101.9 0.0 copy-start.2
  101.9 5.5 %fusion.13 = bf16[384,1024]{1,0:T(8,128)(2,1)} fusion(bf16[1,1024,2048]{2,1,0:T(8,128)(2,1)} %param.8, bf16[1,384,2048]{2,1,0:T(8,128)(2,1)} %all-gather.3.cloned.1.call-done, f32[]{:T(128)S(6)} %div.8), kind=kOutput, calls=%fused_computation.16 | convolution fusion | flops 1613365248 | bytes 6553604 | tf_op jit(solution)/shard_map/ltd,lfd->tf/dot_general | solution.py:36
  107.3 0.0 all-reduce.3.cloned.1.call-update
  107.4 0.0 copy-done.1
  107.4 0.1 copy.10
  107.5 6.9 %fusion = pred[384,1024]{1,0:T(8,128)(4,1)S(1)} fusion(s32[384,32]{1,0:T(8,128)S(1)} %copy.10), kind=kLoop, calls=%fused_computation.1 | loop fusion | flops 24772608 | bytes 442368 | tf_op jit(solution)/shard_map/reduce_or | solution.py:24
  114.5 34.3 %all-reduce.3.cloned.1.call-done = (bf16[384,1024]{1,0:T(8,128)(2,1)}, bf16[384,1024]{1,0:T(8,128)(2,1)}) async-done(((bf16[384,1024]{1,0:T(8,128)(2,1)}, bf16[384,1024]{1,0:T(8,128)(2,1)}), (bf16[384,1024]{1,0:T(8,128)(2,1)}, bf16[384,1024]{1,0:T(8,128)(2,1)})) %all-reduce.3.cloned.1.call-update) | async-done | bytes 1572880 | tf_op jit(solution)/shard_map/psum | solution.py:30
  148.8 0.0 copy-done.2
  148.8 5.5 %convert_bitcast_fusion.1 = bf16[1,1024,2048]{1,2,0:T(8,128)(2,1)} fusion(bf16[1,384,2048]{2,1,0:T(8,128)(2,1)S(1)} %copy-done.2, f32[]{:T(128)S(6)} %div.8, pred[384,1024]{1,0:T(8,128)(4,1)S(1)} %fusion, bf16[384,1024]{1,0:T(8,128)(2,1)} %get-tuple-element.6), kind=kOutput, calls=%fused_computation.7 | convolution fusion | flops 1616248832 | bytes 6946820 | tf_op jit(solution)/shard_map/tf,ltd->lfd/dot_general | solution.py:33
  154.3 0.0 copy-start
  154.3 0.0 copy-start.3
  154.3 6.6 %copy.11 = bf16[1,1024,2048]{2,1,0:T(8,128)(2,1)} copy(bf16[1,1024,2048]{1,2,0:T(8,128)(2,1)} %convert_bitcast_fusion.1) | data formatting | bytes 8388608
  160.9 0.0 copy-done
  160.9 0.0 copy-done.3
  160.9 4.3 %convert_bitcast_fusion = bf16[1,2048,1024]{1,2,0:T(8,128)(2,1)} fusion(bf16[1,384,2048]{2,1,0:T(8,128)(2,1)S(1)} %copy-done, pred[384,1024]{1,0:T(8,128)(4,1)S(1)} %fusion, bf16[384,1024]{1,0:T(8,128)(2,1)S(1)} %copy-done.3), kind=kOutput, calls=%fused_computation.6 | convolution fusion | flops 1613889536 | bytes 6946816 | tf_op jit(solution)/shard_map/ltd,tf->ldf/dot_general | solution.py:39
  165.3 6.4 %copy.12 = bf16[1,2048,1024]{2,1,0:T(8,128)(2,1)} copy(bf16[1,2048,1024]{1,2,0:T(8,128)(2,1)} %convert_bitcast_fusion) | data formatting | bytes 8388608
  (1 shorter events, 0.0 us)
Async XLA Ops:
  7.2 49.9 %all-gather.5.cloned.1.call-start = ((), (), s32[]{:S(2)}) async-start(), calls=%async_computation.1 | async-start | bytes 1769472 | tf_op jit(solution)/shard_map/all_gather | solution.py:14
  7.9 94.0 %all-gather.3.cloned.1.call-start = ((), (), s32[]{:S(2)}) async-start(), calls=%async_computation | async-start | bytes 1769472 | tf_op jit(solution)/shard_map/all_gather | solution.py:15
  8.6 140.1 %all-reduce.3.cloned.1.call-start = ((), (), s32[]{:S(2)}) async-start(), calls=%async_computation.2 | async-start | bytes 3145728 | tf_op jit(solution)/shard_map/psum | solution.py:30
  65.9 41.4 %copy-start.1 = (s32[384,32]{0,1:T(8,128)S(1)}, s32[384,32]{0,1:T(8,128)}, u32[]{:S(2)}) copy-start(s32[384,32]{0,1:T(8,128)} %param.9) | copy-start | bytes 147460
  101.9 46.9 %copy-start.2 = (bf16[1,384,2048]{2,1,0:T(8,128)(2,1)S(1)}, bf16[1,384,2048]{2,1,0:T(8,128)(2,1)}, u32[]{:S(2)}) copy-start(bf16[1,384,2048]{2,1,0:T(8,128)(2,1)} %all-gather.3.cloned.1.call-done) | copy-start | bytes 4718596
  154.3 6.6 %copy-start = (bf16[1,384,2048]{2,1,0:T(8,128)(2,1)S(1)}, bf16[1,384,2048]{2,1,0:T(8,128)(2,1)}, u32[]{:S(2)}) copy-start(bf16[1,384,2048]{2,1,0:T(8,128)(2,1)} %all-gather.5.cloned.1.call-done) | copy-start | bytes 4718596
  154.3 6.6 %copy-start.3 = (bf16[384,1024]{1,0:T(8,128)(2,1)S(1)}, bf16[384,1024]{1,0:T(8,128)(2,1)}, u32[]{:S(2)}) copy-start(bf16[384,1024]{1,0:T(8,128)(2,1)} %get-tuple-element.7) | copy-start | bytes 2359300
Sparse Core Ops, SparseCore 0:
  10.2 46.8 all-gather.4
  59.3 42.5 all-gather.2
  107.5 41.2 all-reduce.2
where the time goes:
time: 179 us; the launch traced here: 178 us
  waiting for transfers between devices  120 us (67%)
  matrix products  20.7 us (12%)
  between operations  14.5 us (8%)
  local copies, waits for them, and re-layouts  13.1 us (7%)
  other arithmetic  9.77 us (5%)
    all_gather x1, waiting for transfers between devices, on_device(): lax.all_gather(acts, 'feat', axis=1, tiled=True)  48.4 us
    all_gather x1, waiting for transfers between devices, on_device(): lax.all_gather(errors, 'feat', axis=1, tiled=True)  35.9 us
    psum x1, waiting for transfers between devices, on_device(): lax.psum(partial_value.astype(jnp.bfloat16), 'layer').astype(jnp.float32)  34.3 us
    unnamed x10, local copies, waits for them, and re-layouts  13 us
    reduce_or x1, other arithmetic, on_device(): mask = jnp.any(slot_match(target, feat_dev), axis=1).astype(jnp.float32)  6.93 us
    dot_general x1, matrix products, on_device(): jnp.einsum('tf,ltd->lfd', codes, delta, preferred_element_type=jnp.float32)  5.55 us
    dot_general x1, matrix products, on_device(): jnp.einsum('ltd,lfd->tf', delta, dec_weight, preferred_element_type=jnp.f...  5.49 us
    dot_general x1, matrix products, on_device(): jnp.einsum('ltd,ldf->tf', all_acts, enc_weight, preferred_element_type=jn...  5.34 us
  transfers between devices with their start and end apart: 3, of which 3 were waited for; matrix products, arithmetic and copies ran while one was open for 9% of the time, Pallas kernels for 0%

commit v1 on v0

--- a/solution.py
+++ b/solution.py
@@ -2,6 +2,7 @@
 import jax.numpy as jnp
 from jax import lax
 from jax.sharding import PartitionSpec as P
+from jax.lax import all_gather
 
 
 def slot_match(target, feat_dev):
@@ -27,7 +28,7 @@
     partial_value = jnp.einsum(
         "ltd,ldf->tf", all_acts, enc_weight, preferred_element_type=jnp.float32
     )
-    pre = lax.psum(partial_value.astype(jnp.bfloat16), "layer").astype(jnp.float32)
+    pre = all_gather(partial_value.astype(jnp.bfloat16), "layer").sum(axis=0).astype(jnp.float32)
     codes = (pre * mask).astype(jnp.bfloat16)
     delta = (all_errors.astype(jnp.float32) * scale[:, None, None]).astype(jnp.bfloat16)
     dec_grad = jnp.einsum("tf,ltd->lfd", codes, delta, preferred_element_type=jnp.float32).astype(

time: 179 us -> 191 us (1.067)
  waiting for transfers between devices: 120 us -> 130 us
  other arithmetic: 9.77 us -> 12.3 us
    all_gather x0 -> x1, waiting for transfers between devices: none -> 17.9 us  [on_device(): all_gather(partial_value.astype(jnp.bfloat16), 'layer').sum(axis=0)]
    psum x1, waiting for transfers between devices: 34.3 us -> 21.5 us  [on_device(): lax.psum(grad_partial.astype(jnp.bfloat16), 'layer').astype(jnp.float32)]
    all_gather x1, waiting for transfers between devices: 35.9 us -> 41.2 us  [on_device(): lax.all_gather(errors, 'feat', axis=1, tiled=True)]
    reduce_sum x0 -> x1, other arithmetic: none -> 2.58 us  [on_device(): all_gather(partial_value.astype(jnp.bfloat16), 'layer').sum(axis=0)]
    unnamed x10 -> x8, local copies, waits for them, and re-layouts: 13 us -> 13 us
  transfers between devices with their start and end apart: 3 -> 4, of which waited for: 3 -> 4; matrix products, arithmetic and copies ran while one was open for 9% -> 14% of each run, Pallas kernels for 0% -> 0%
where the time goes in v1:
time: 191 us
  waiting for transfers between devices  130 us (68%)
  matrix products  20.1 us (11%)
  between operations  14.5 us (8%)
  local copies, waits for them, and re-layouts  13.1 us (7%)
  other arithmetic  12.3 us (6%)
    all_gather x1, waiting for transfers between devices, on_device(): lax.all_gather(acts, 'feat', axis=1, tiled=True)  48.4 us
    all_gather x1, waiting for transfers between devices, on_device(): lax.all_gather(errors, 'feat', axis=1, tiled=True)  41.2 us
    psum x1, waiting for transfers between devices, on_device(): lax.psum(grad_partial.astype(jnp.bfloat16), 'layer').astype(jnp.float32)  21.5 us
    all_gather x1, waiting for transfers between devices, on_device(): all_gather(partial_value.astype(jnp.bfloat16), 'layer').sum(axis=0)  17.9 us
    unnamed x8, local copies, waits for them, and re-layouts  13 us
    reduce_or x1, other arithmetic, on_device(): mask = jnp.any(slot_match(target, feat_dev), axis=1).astype(jnp.float32)  6.93 us
    dot_general x1, matrix products, on_device(): jnp.einsum('ltd,tf->ldf', all_acts, pre_grad, preferred_element_type=jnp....  5.54 us
    dot_general x1, matrix products, on_device(): jnp.einsum('ltd,lfd->tf', delta, dec_weight, preferred_element_type=jnp.f...  5.37 us
  transfers between devices with their start and end apart: 4, of which 4 were waited for; matrix products, arithmetic and copies ran while one was open for 14% of the time, Pallas kernels for 0%

profile of v1, /device:TPU:0, one launch (start us, length us, event | category | flops | bytes accessed | tf_op | source)
XLA Modules:
  0.0 190.7 jit_solution(6892999027449176999)
XLA Ops:
  7.2 0.0 all-gather.7.cloned.1.call-start
  7.2 0.7 all-gather.7.cloned.1.call-update
  7.9 0.0 all-gather.5.cloned.1.call-start
  7.9 0.7 all-gather.5.cloned.1.call-update
  8.6 0.0 all-reduce.2.cloned.1.call-start
  8.7 48.4 %all-gather.7.cloned.1.call-done = bf16[1,384,2048]{2,1,0:T(8,128)(2,1)} async-done(((bf16[1,48,2048]{2,1,0:T(8,128)(2,1)}), bf16[1,384,2048]{2,1,0:T(8,128)(2,1)}) %all-gather.7.cloned.1.call-update) | async-done | bytes 1572880 | tf_op jit(solution)/shard_map/all_gather | solution.py:15
  57.1 2.8 %multiply_reduce_fusion = f32[]{:T(128)} fusion(bf16[1,384,2048]{2,1,0:T(8,128)(2,1)} %all-gather.7.cloned.1.call-done), kind=kLoop, calls=%fused_computation.9 | loop fusion | flops 2359295 | bytes 1572868 | tf_op jit(solution)/shard_map/reduce_sum | solution.py:26
  60.6 0.0 copy-start
  60.6 41.2 %all-gather.5.cloned.1.call-done = bf16[1,384,2048]{2,1,0:T(8,128)(2,1)} async-done(((bf16[1,48,2048]{2,1,0:T(8,128)(2,1)}), bf16[1,384,2048]{2,1,0:T(8,128)(2,1)}) %all-gather.5.cloned.1.call-update) | async-done | bytes 1572880 | tf_op jit(solution)/shard_map/all_gather | solution.py:16
  101.8 5.4 %fusion.13 = bf16[384,1024]{1,0:T(8,128)(2,1)} fusion(bf16[1,1024,2048]{2,1,0:T(8,128)(2,1)} %param.8, bf16[1,384,2048]{2,1,0:T(8,128)(2,1)} %all-gather.5.cloned.1.call-done, f32[]{:T(128)S(6)} %div.8), kind=kOutput, calls=%fused_computation.16 | convolution fusion | flops 1613365248 | bytes 6553604 | tf_op jit(solution)/shard_map/ltd,lfd->tf/dot_general | solution.py:37
  107.2 0.0 all-reduce.2.cloned.1.call-update
  107.2 0.0 copy-start.1
  107.3 0.0 all-gather.9.cloned.1.call-start
  107.3 0.0 copy-done
  107.3 4.9 %fusion.8 = bf16[384,1024]{1,0:T(8,128)(2,1)} fusion(bf16[1,2048,1024]{2,1,0:T(8,128)(2,1)} %param.7, bf16[1,384,2048]{2,1,0:T(8,128)(2,1)S(1)} %copy-done), kind=kOutput, calls=%fused_computation.15 | convolution fusion | flops 1611005952 | bytes 6553600 | tf_op jit(solution)/shard_map/ltd,ldf->tf/dot_general | solution.py:28
  112.2 0.0 all-gather.9.cloned.1.call-update
  112.2 0.0 copy-done.1
  112.2 0.1 copy.10
  112.4 6.9 %fusion = pred[384,1024]{1,0:T(8,128)(4,1)S(1)} fusion(s32[384,32]{1,0:T(8,128)S(1)} %copy.10), kind=kLoop, calls=%fused_computation.1 | loop fusion | flops 24772608 | bytes 442368 | tf_op jit(solution)/shard_map/reduce_or | solution.py:25
  119.3 21.5 %all-reduce.2.cloned.1.call-done = bf16[384,1024]{1,0:T(8,128)(2,1)} async-done(((bf16[384,1024]{1,0:T(8,128)(2,1)}), bf16[384,1024]{1,0:T(8,128)(2,1)}) %all-reduce.2.cloned.1.call-update) | async-done | bytes 786448 | tf_op jit(solution)/shard_map/psum | solution.py:38
  140.8 5.5 %convert_bitcast_fusion = bf16[1,2048,1024]{1,2,0:T(8,128)(2,1)} fusion(bf16[1,384,2048]{2,1,0:T(8,128)(2,1)S(1)} %copy-done, pred[384,1024]{1,0:T(8,128)(4,1)S(1)} %fusion, bf16[384,1024]{1,0:T(8,128)(2,1)} %all-reduce.2.cloned.1.call-done), kind=kOutput, calls=%fused_computation.6 | convolution fusion | flops 1613889536 | bytes 6946816 | tf_op jit(solution)/shard_map/ltd,tf->ldf/dot_general | solution.py:40
  146.3 6.5 %copy.12 = bf16[1,2048,1024]{2,1,0:T(8,128)(2,1)} copy(bf16[1,2048,1024]{1,2,0:T(8,128)(2,1)} %convert_bitcast_fusion) | data formatting | bytes 8388608
  152.9 0.0 copy-start.2
  152.9 17.9 %all-gather.9.cloned.1.call-done = bf16[1536,1024]{1,0:T(8,128)(2,1)} async-done(((bf16[384,1024]{1,0:T(8,128)(2,1)}), bf16[1536,1024]{1,0:T(8,128)(2,1)}) %all-gather.9.cloned.1.call-update) | async-done | bytes 3145744 | tf_op jit(solution)/shard_map/all_gather | solution.py:31
  170.8 2.6 %reduce_sum.22 = bf16[384,1024]{1,0:T(8,128)(2,1)S(1)} reduce(bf16[4,384,1024]{2,1,0:T(8,128)(2,1)} %bitcast.30, bf16[]{:T(256)} %constant.26.clone.1), dimensions={0}, to_apply=%region_2.3 | reduce | flops 1179648 | bytes 3932162 | tf_op jit(solution)/shard_map/reduce_sum | solution.py:31
  173.3 0.0 copy-done.2
  173.3 4.3 %convert_bitcast_fusion.1 = bf16[1,1024,2048]{1,2,0:T(8,128)(2,1)} fusion(bf16[1,384,2048]{2,1,0:T(8,128)(2,1)S(1)} %copy-done.2, f32[]{:T(128)S(6)} %div.8, pred[384,1024]{1,0:T(8,128)(4,1)S(1)} %fusion, bf16[384,1024]{1,0:T(8,128)(2,1)S(1)} %reduce_sum.22), kind=kOutput, calls=%fused_computation.7 | convolution fusion | flops 1616248832 | bytes 6946820 | tf_op jit(solution)/shard_map/tf,ltd->lfd/dot_general | solution.py:34
  177.7 6.4 %copy.11 = bf16[1,1024,2048]{2,1,0:T(8,128)(2,1)} copy(bf16[1,1024,2048]{1,2,0:T(8,128)(2,1)} %convert_bitcast_fusion.1) | data formatting | bytes 8388608
  (1 shorter events, 0.0 us)
Async XLA Ops:
  7.2 49.9 %all-gather.7.cloned.1.call-start = ((), (), s32[]{:S(2)}) async-start(), calls=%async_computation.1 | async-start | bytes 1769472 | tf_op jit(solution)/shard_map/all_gather | solution.py:15
  7.9 93.9 %all-gather.5.cloned.1.call-start = ((), (), s32[]{:S(2)}) async-start(), calls=%async_computation | async-start | bytes 1769472 | tf_op jit(solution)/shard_map/all_gather | solution.py:16
  8.6 132.1 %all-reduce.2.cloned.1.call-start = ((), (), s32[]{:S(2)}) async-start(), calls=%async_computation.2 | async-start | bytes 1572864 | tf_op jit(solution)/shard_map/psum | solution.py:38
  60.6 46.7 %copy-start = (bf16[1,384,2048]{2,1,0:T(8,128)(2,1)S(1)}, bf16[1,384,2048]{2,1,0:T(8,128)(2,1)}, u32[]{:S(2)}) copy-start(bf16[1,384,2048]{2,1,0:T(8,128)(2,1)} %all-gather.7.cloned.1.call-done) | copy-start | bytes 4718596
  107.2 5.0 %copy-start.1 = (s32[384,32]{0,1:T(8,128)S(1)}, s32[384,32]{0,1:T(8,128)}, u32[]{:S(2)}) copy-start(s32[384,32]{0,1:T(8,128)} %param.9) | copy-start | bytes 147460
  107.3 63.5 %all-gather.9.cloned.1.call-start = ((), (), s32[]{:S(2)}) async-start(), calls=%async_computation.3 | async-start | bytes 3932160 | tf_op jit(solution)/shard_map/all_gather | solution.py:31
  152.9 20.5 %copy-start.2 = (bf16[1,384,2048]{2,1,0:T(8,128)(2,1)S(1)}, bf16[1,384,2048]{2,1,0:T(8,128)(2,1)}, u32[]{:S(2)}) copy-start(bf16[1,384,2048]{2,1,0:T(8,128)(2,1)} %all-gather.5.cloned.1.call-done) | copy-start | bytes 4718596
Sparse Core Ops, SparseCore 0:
  10.2 46.8 all-gather.6
  59.3 42.5 all-gather.4
  107.4 33.3 all-reduce.1
  142.2 28.4 all-gather.8
